TPU v7x, 256 devices: a whole 4x4x8 slice. The times are simulated.
256 devices in a mesh: row: 32 (over z, y_hi, core), col: 8 (over x, y_lo).
Axes of the slice: x: 4, y: 4 (y_hi: 2, y_lo: 2; y = y_hi * 2 + y_lo), z: 8, core: 2. Of those that a mesh axis runs over, the one named last changes fastest.
Arguments:
- currents: float32 [8, 131072], P(None, ('row', 'col')), may hold values from -6 to 6
- src_pos: float32 [3, 131072], P(None, ('row', 'col')), may hold values from 0 to 1
- src_dir: float32 [3, 131072], P(None, ('row', 'col')), may hold values from -1 to 1
- cell_ends: int32 [2, 131072], P(None, ('row', 'col')), may hold values from 0 to 65535, as said below
- pan_pos: float32 [3, 65536], P(None, ('row', 'col')), may hold values from 0 to 1
- tgt_pos: float32 [3, 8192], P(None, 'row'), may hold values from 0 to 1
- tgt_dir: float32 [3, 8192], P(None, 'row'), may hold values from -1 to 1
- tgt_ends: int32 [2, 8192], P(None, 'row'), may hold values from 0 to 4095, as said below
- wpan_pos: float32 [3, 4096], P(None, 'row'), may hold values from 0 to 1
Outputs:
- voltage: float32 [8, 8192], P(None, ('row', 'col'))
Inputs may be any that keep to these rules, and one draw needn't show every extreme that they name: `cell_ends`: A cell's two panels differ. Source cell j and its panels belong to devices with the same col index: with b = j // 512 and c = p // 256, b and c leave the same remainder on division by 8. `tgt_ends`: A target cell's two panels differ.
All inputs are finite; a program needn't handle non-finite values.
Results may differ from a plain program's by a relative error of at most 0.006.
Values may be sent and summed in bfloat16 or wider, within the bound.
No kernel may reach another device: no remote copies, remote signals or barrier semaphores. Data moves between devices by JAX's collectives and lax.ppermute only.
A program may use at most 64 MiB of HBM per device.

v0:
```python
import math
import jax
import jax.numpy as jnp
from jax import lax
from jax.sharding import PartitionSpec as P

CELLS = 131072
PANELS = 65536
soft_sq = 0.0004
wave_num = 12.0


def kernel_tile(tpos, spos, tdir, sdir):
    dx = tpos[0][:, None] - spos[0][None, :]
    dy = tpos[1][:, None] - spos[1][None, :]
    dz = tpos[2][:, None] - spos[2][None, :]
    dist_sq = dx * dx + dy * dy + dz * dz + soft_sq
    inverse = lax.rsqrt(dist_sq)
    phase = wave_num * dist_sq * inverse
    real_part = jnp.cos(phase) * inverse
    imag_part = -jnp.sin(phase) * inverse
    if tdir is not None:
        inner = (
            tdir[0][:, None] * sdir[0][None, :]
            + tdir[1][:, None] * sdir[1][None, :]
            + tdir[2][:, None] * sdir[2][None, :]
        )
        real_part = real_part * inner
        imag_part = imag_part * inner
    return jnp.concatenate([real_part, imag_part], axis=1).astype(jnp.bfloat16)


def apply_tile(stacked, source):
    half = source.shape[0] // 2
    real_src = source[:half]
    imag_src = source[half:]
    left = jnp.concatenate(
        [jnp.concatenate([real_src, -imag_src], 1), jnp.concatenate([imag_src, real_src], 1)], 0
    )
    return lax.dot_general(
        left, stacked, (((1,), (1,)), ((), ())), preferred_element_type=jnp.float32
    )


def sweep(tpos, tdir, spos, sdir, source):
    length = spos.shape[1]
    width = min(length, 2048)
    total = None
    for block in range(length // width):
        lower = block * width
        upper = lower + width
        sub_dir = None if sdir is None else sdir[:, lower:upper]
        term = apply_tile(
            kernel_tile(tpos, spos[:, lower:upper], tdir, sub_dir), source[:, lower:upper]
        )
        total = term if total is None else total + term
    return total


def per_device(
    currents, src_pos, src_dir, cell_ends, pan_pos, tgt_pos, tgt_dir, tgt_ends, wpan_pos
):
    doubled = currents.shape[0]
    half = doubled // 2
    col_count = lax.axis_size("col")
    col_index = lax.axis_index("col")
    panel_dev = pan_pos.shape[1]
    block_len = panel_dev * lax.axis_size("row")
    cur16 = currents.astype(jnp.bfloat16)
    cur_all = lax.all_gather(cur16, "row", axis=1, tiled=True)
    charge_zero = jnp.zeros((doubled, block_len), jnp.float32)
    spos = lax.all_gather(src_pos, "row", axis=1, tiled=True)
    sdir = lax.all_gather(src_dir, "row", axis=1, tiled=True)
    source = cur_all
    induct = sweep(tgt_pos, tgt_dir, spos, sdir, source)
    cur_wide = cur16.astype(jnp.float32)
    local_ends = cell_ends // (panel_dev * col_count) * panel_dev + cell_ends % panel_dev
    partial_value = (
        charge_zero.at[:, local_ends[0]].add(cur_wide).at[:, local_ends[1]].add(-cur_wide)
    )
    q16 = lax.psum(partial_value, "row").astype(jnp.bfloat16)
    source = q16
    field = sweep(wpan_pos, None, lax.all_gather(pan_pos, "row", axis=1, tiled=True), None, source)
    share = tgt_pos.shape[1] // col_count
    induct_all, field_all = lax.psum((induct, field), "col")
    induct_mine = lax.dynamic_slice_in_dim(induct_all, col_index * share, share, 1)
    pscale = 0.25 / math.sqrt(PANELS)
    lscale = 1.0 / math.sqrt(CELLS)
    potential_part = jnp.concatenate([field_all[half:], -field_all[:half]], 0) * pscale
    potential = lax.all_gather(potential_part, "row", axis=1, tiled=True)
    voltage = jnp.concatenate([-induct_mine[half:], induct_mine[:half]], 0) * lscale
    my_ends = lax.dynamic_slice_in_dim(tgt_ends, col_index * share, share, 1)
    return (
        voltage + jnp.take(potential, my_ends[0], axis=1) - jnp.take(potential, my_ends[1], axis=1)
    )


def solution(mesh):
    return jax.shard_map(
        per_device,
        mesh=mesh,
        in_specs=(
            P(None, ("row", "col")),
            P(None, ("row", "col")),
            P(None, ("row", "col")),
            P(None, ("row", "col")),
            P(None, ("row", "col")),
            P(None, "row"),
            P(None, "row"),
            P(None, "row"),
            P(None, "row"),
        ),
        out_specs=P(None, ("row", "col")),
        check_vma=False,
    )
```

profile of v0, /device:TPU:1, one launch (start us, length us, event | category | flops | bytes accessed | tf_op | source)
XLA Modules:
  0.0 485.7 jit_solution(14335581508458441248)
XLA Ops:
  0.0 0.0 copy-start
  0.0 0.0 copy-start.2
  0.0 0.0 copy-start.1
  0.0 0.7 copy-done
  0.7 0.1 constant_dynamic-slice_fusion
  0.8 0.8 slice_bitcast_fusion.4
  1.6 0.8 fusion.175
  2.4 0.8 fusion.176
  3.2 0.7 fusion.153
  3.9 0.7 fusion.152
  4.6 46.7 %all_gather.18 = f32[3,8192]{1,0:T(4,128)S(1)} all-gather(f32[3,256]{1,0:T(4,128)} %param.15), channel_id=1, replica_groups=mesh['row'=32,'col'=8] {'row'}, dimensions={1}, use_global_device_ids=true | all-gather | bytes 101376 | tf_op jit(solution)/shard_map/all_gather | solution.py:83
  51.4 0.1 fusion.173
  51.5 0.1 copy.44
  51.6 0.1 copy.45
  51.7 37.4 %all_gather.15 = bf16[8,16384]{1,0:T(8,128)(2,1)S(1)} all-gather(bf16[8,512]{1,0:T(8,128)(2,1)S(1)} %get-tuple-element.13), channel_id=1, replica_groups=mesh['row'=32,'col'=8] {'row'}, dimensions={1}, use_global_device_ids=true | all-gather | bytes 270336 | tf_op jit(solution)/shard_map/all_gather | solution.py:70
  89.2 0.1 slice_negate_fusion.6
  89.3 0.0 copy-done.1
  89.3 40.3 %all_gather.16 = f32[3,16384]{1,0:T(4,128)S(1)} all-gather(f32[3,512]{1,0:T(4,128)S(1)} %copy-done.1), channel_id=1, replica_groups=mesh['row'=32,'col'=8] {'row'}, dimensions={1}, use_global_device_ids=true | all-gather | bytes 202752 | tf_op jit(solution)/shard_map/all_gather | solution.py:72
  129.6 0.1 fusion.168
  129.8 0.0 copy-done.2
  129.8 37.4 %all_gather.17 = f32[3,16384]{1,0:T(4,128)S(1)} all-gather(f32[3,512]{1,0:T(4,128)S(1)} %copy-done.2), channel_id=1, replica_groups=mesh['row'=32,'col'=8] {'row'}, dimensions={1}, use_global_device_ids=true | all-gather | bytes 202752 | tf_op jit(solution)/shard_map/all_gather | solution.py:73
  167.2 0.1 fusion.169
  167.3 4.4 scatter_custom_fusion
  171.8 7.1 %scatter_fusion = f32[8,8192]{0,1:T(8,128)} fusion(f32[8,8192]{0,1:T(8,128)} %scatter_custom_fusion, s32[512]{0:T(512)S(1)} %bitcast.96, f32[512,8]{1,0:T(8,128)S(1)} %copy.45), kind=kCustom, calls=%fused_computation.3 | custom fusion | flops 4096 | bytes 51200 | tf_op jit(solution)/shard_map/scatter-add | solution.py:79
  178.9 2.8 copy.46
  181.7 127.5 %all-reduce.2 = bf16[8,8192]{1,0:T(8,128)(2,1)S(1)} all-reduce(f32[8,8192]{1,0:T(8,128)S(1)} %copy.46), channel_id=1, replica_groups=mesh['row'=32,'col'=8] {'row'}, use_global_device_ids=true, to_apply=%region_3.4 | all-reduce | flops 65536 | bytes 393216 | tf_op jit(solution)/shard_map/psum | solution.py:81
  309.1 0.1 slice_negate_fusion.2
  309.2 17.0 %multiply_convert_fusion.17 = (bf16[128,2048]{1,0:T(8,128)(2,1)S(1)}, bf16[128,2048]{1,0:T(8,128)(2,1)S(1)}, bf16[128,2048]{1,0:T(8,128)(2,1)S(1)}, bf16[128,204...) fusion(f32[2048]{0:T(1024)S(1)} %bitcast.128, ...), kind=kLoop, calls=%fused_computation.102 | loop fusion | flops 16777216 | bytes 4294144 | tf_op jit(solution)/shard_map/convert
  326.2 0.4 fusion.55
  326.6 0.4 convolution_add_fusion.2
  327.0 0.4 convolution_add_fusion.1
  327.4 0.4 convolution_add_fusion
  327.8 18.5 %multiply_convert_fusion.1 = (bf16[256,2048]{1,0:T(8,128)(2,1)S(1)}, bf16[256,2048]{1,0:T(8,128)(2,1)S(1)}, bf16[256,2048]{1,0:T(8,128)(2,1)S(1)}, bf16[256,2048]{1,0:T(8,128)(2,1)S(1)}) fusion(f32[2048]{0:T(1024)S(1)} %bitcast.154, f32[2048]{0:T(1024)S(1)} %bitcast.155, f32[2048]{0:T(1024)S(1)} %bitcast.153, f32[2048]{0:T(1024)S(1)} %bitcast.142, ...), kind=kLoop, calls=%fused_computation.39 | loop fusion | flops 24117248 | bytes 4298752 | tf_op jit(solution)/shard_map/convert.8
  346.3 18.3 %multiply_convert_fusion.7 = (bf16[256,2048]{1,0:T(8,128)(2,1)S(1)}, bf16[256,2048]{1,0:T(8,128)(2,1)S(1)}, bf16[256,2048]{1,0:T(8,128)(2,1)S(1)}, bf16[256,2048]{1,0:T(8,128)(2,1)S(1)}) fusion(f32[2048]{0:T(1024)S(1)} %bitcast.148, f32[2048]{0:T(1024)S(1)} %bitcast.149, f32[2048]{0:T(1024)S(1)} %bitcast.150, f32[2048]{0:T(1024)S(1)} %bitcast.124, ...), kind=kLoop, calls=%fused_computation.54 | loop fusion | flops 24117248 | bytes 4298752 | tf_op jit(solution)/shard_map/convert.14
  364.6 0.6 fusion
  365.2 0.7 fusion.52
  365.9 18.3 %multiply_convert_fusion.3 = (bf16[256,2048]{1,0:T(8,128)(2,1)S(1)}, bf16[256,2048]{1,0:T(8,128)(2,1)S(1)}, bf16[256,2048]{1,0:T(8,128)(2,1)S(1)}, bf16[256,2048]{1,0:T(8,128)(2,1)S(1)}) fusion(f32[2048]{0:T(1024)S(1)} %bitcast.118, f32[2048]{0:T(1024)S(1)} %bitcast.119, f32[2048]{0:T(1024)S(1)} %bitcast.120, f32[2048]{0:T(1024)S(1)} %bitcast.109, ...), kind=kLoop, calls=%fused_computation.44 | loop fusion | flops 24117248 | bytes 4298752 | tf_op jit(solution)/shard_map/convert.10
  384.2 0.6 fusion.49
  384.8 18.3 %multiply_convert_fusion.5 = (bf16[256,2048]{1,0:T(8,128)(2,1)S(1)}, bf16[256,2048]{1,0:T(8,128)(2,1)S(1)}, bf16[256,2048]{1,0:T(8,128)(2,1)S(1)}, bf16[256,2048]{1,0:T(8,128)(2,1)S(1)}) fusion(f32[2048]{0:T(1024)S(1)} %bitcast.103, f32[2048]{0:T(1024)S(1)} %bitcast.104, f32[2048]{0:T(1024)S(1)} %bitcast.105, f32[2048]{0:T(1024)S(1)} %bitcast.97, ...), kind=kLoop, calls=%fused_computation.49 | loop fusion | flops 24117248 | bytes 4298752 | tf_op jit(solution)/shard_map/convert.12
  403.1 0.6 fusion.46
  403.8 0.7 fusion.43
  404.4 0.7 fusion.40
  405.1 0.7 fusion.37
  405.8 0.7 fusion.34
  406.4 26.1 %all-reduce = (f32[8,256]{1,0:T(8,128)S(1)}, f32[8,128]{1,0:T(8,128)S(1)}) all-reduce(f32[8,256]{1,0:T(8,128)S(1)} %fusion.34, f32[8,128]{1,0:T(8,128)S(1)} %convolution_add_fusion), channel_id=1, replica_groups=mesh['row'=32,'col'=8] {'col'}, use_global_device_ids=true, to_apply=%region_0.1 | all-reduce | flops 3072 | bytes 24576 | tf_op jit(solution)/shard_map/psum | solution.py:85
  432.5 0.1 constant_dynamic-slice_fusion.1
  432.6 50.1 %all_gather.19 = f32[8,4096]{1,0:T(8,128)S(1)} all-gather(f32[8,128]{1,0:T(8,128)S(1)} %maximum_multiply_fusion.1), channel_id=1, replica_groups=mesh['row'=32,'col'=8] {'row'}, dimensions={1}, use_global_device_ids=true | all-gather | bytes 135168 | tf_op jit(solution)/shard_map/all_gather | solution.py:90
  482.7 0.6 copy.47
  483.3 0.6 gather_fusion.1
  483.9 0.6 gather_fusion
  484.5 0.1 copy.48
  484.6 0.1 copy.50
  484.6 0.6 fusion.155
  (10 shorter events, 0.1 us)
Async XLA Ops:
  0.0 0.7 copy-start
  0.0 129.8 %copy-start.2 = (f32[3,512]{1,0:T(4,128)S(1)}, f32[3,512]{1,0:T(4,128)}, u32[]{:S(2)}) copy-start(f32[3,512]{1,0:T(4,128)} %param.13) | copy-start | bytes 18436
  0.0 89.3 %copy-start.1 = (f32[3,512]{1,0:T(4,128)S(1)}, f32[3,512]{1,0:T(4,128)}, u32[]{:S(2)}) copy-start(f32[3,512]{1,0:T(4,128)} %param.12) | copy-start | bytes 18436
where the time goes:
time: 491 us; the launch traced here: 486 us
  blocking collectives  366 us (75%)
  other arithmetic  104 us (21%)
  local copies, waits for them, and re-layouts  8.52 us (2%)
  matrix products  6.77 us (1%)
    psum x1, blocking collectives, per_device(): q16 = lax.psum(partial_value, 'row').astype(jnp.bfloat16)  127 us
    another operation x5, other arithmetic  90.4 us
    all_gather x1, blocking collectives, per_device(): potential = lax.all_gather(potential_part, 'row', axis=1, tiled=True)  50.1 us
    all_gather x1, blocking collectives, per_device(): lax.all_gather(pan_pos, 'row', axis=1, tiled=True)  46.7 us
    all_gather x1, blocking collectives, per_device(): spos = lax.all_gather(src_pos, 'row', axis=1, tiled=True)  40.3 us
    all_gather x1, blocking collectives, per_device(): cur_all = lax.all_gather(cur16, 'row', axis=1, tiled=True)  37.4 us
    all_gather x1, blocking collectives, per_device(): sdir = lax.all_gather(src_dir, 'row', axis=1, tiled=True)  37.4 us
    psum x1, blocking collectives, per_device(): induct_all, field_all = lax.psum((induct, field), 'col')  26.1 us

commit v1 on v0

--- a/solution.py
+++ b/solution.py
@@ -8,6 +8,11 @@
 PANELS = 65536
 soft_sq = 0.0004
 wave_num = 12.0
+
+
+def gather_over(array, axis, dim):
+    stack = jnp.stack([array] * lax.axis_size(axis))
+    return jnp.concatenate(lax.all_to_all(stack, axis, 0, 0), axis=dim)
 
 
 def kernel_tile(tpos, spos, tdir, sdir):
@@ -80,7 +85,7 @@
     )
     q16 = lax.psum(partial_value, "row").astype(jnp.bfloat16)
     source = q16
-    field = sweep(wpan_pos, None, lax.all_gather(pan_pos, "row", axis=1, tiled=True), None, source)
+    field = sweep(wpan_pos, None, gather_over(pan_pos, "row", 1), None, source)
     share = tgt_pos.shape[1] // col_count
     induct_all, field_all = lax.psum((induct, field), "col")
     induct_mine = lax.dynamic_slice_in_dim(induct_all, col_index * share, share, 1)

time: 491 us -> 458 us (0.933)
  blocking collectives: 366 us -> 322 us
  starting transfers between devices: 0 us -> 12.7 us
    all_gather x1 -> x0, blocking collectives: 46.7 us -> none  [per_device(): lax.all_gather(pan_pos, 'row', axis=1, tiled=True)]
    all_to_all x0 -> x1, starting transfers between devices: none -> 12.7 us  [gather_over(): return jnp.concatenate(lax.all_to_all(stack, axis, 0, 0), axis=dim)]
    all_gather x1, blocking collectives: 37.4 us -> 42.6 us  [per_device(): cur_all = lax.all_gather(cur16, 'row', axis=1, tiled=True)]
  transfers between devices with their start and end apart: 0 -> 1, of which waited for: 0 -> 0; matrix products, arithmetic and copies ran while one was open for 0% -> 21% of each run, Pallas kernels for 0% -> 0%
where the time goes in v1:
time: 458 us; the launch traced here: 452 us
  blocking collectives  322 us (70%)
  other arithmetic  104 us (23%)
  starting transfers between devices  12.7 us (3%)
  local copies, waits for them, and re-layouts  6.93 us (2%)
  matrix products  6.75 us (1%)
    psum x1, blocking collectives, per_device(): q16 = lax.psum(partial_value, 'row').astype(jnp.bfloat16)  125 us
    another operation x5, other arithmetic  90.5 us
    all_gather x1, blocking collectives, per_device(): potential = lax.all_gather(potential_part, 'row', axis=1, tiled=True)  50.1 us
    all_gather x1, blocking collectives, per_device(): cur_all = lax.all_gather(cur16, 'row', axis=1, tiled=True)  42.6 us
    all_gather x1, blocking collectives, per_device(): sdir = lax.all_gather(src_dir, 'row', axis=1, tiled=True)  40.5 us
    all_gather x1, blocking collectives, per_device(): spos = lax.all_gather(src_pos, 'row', axis=1, tiled=True)  37.7 us
    psum x1, blocking collectives, per_device(): induct_all, field_all = lax.psum((induct, field), 'col')  26.1 us
    all_to_all x1, starting transfers between devices, gather_over(): return jnp.concatenate(lax.all_to_all(stack, axis, 0, 0), axis=dim)  12.7 us
  transfers between devices with their start and end apart: 1, of which 0 were waited for; matrix products, arithmetic and copies ran while one was open for 21% of the time, Pallas kernels for 0%

profile of v1, /device:TPU:1, one launch (start us, length us, event | category | flops | bytes accessed | tf_op | source)
XLA Modules:
  0.0 452.5 jit_solution(6560582510954744041)
XLA Ops:
  0.0 0.0 copy-start
  0.0 0.0 copy-start.2
  0.0 0.0 copy-start.3
  0.0 0.0 copy-start.1
  0.0 1.4 stack.2
  1.4 12.7 %all-to-all-start = ((f32[32,3,256]{2,1,0:T(4,128)}), f32[32,3,256]{2,1,0:T(4,128)S(1)}, u32[]{:S(2)}, u32[]{:S(2)}) async-start(f32[32,3,256]{2,1,0:T(4,128)} %stack.2), calls=%async_computation | async-start | bytes 262144 | tf_op jit(solution)/shard_map/all_to_all | solution.py:15
  14.2 0.7 fusion.152
  14.9 42.6 %all_gather.12 = bf16[8,16384]{1,0:T(8,128)(2,1)S(1)} all-gather(bf16[8,512]{1,0:T(8,128)(2,1)S(1)} %get-tuple-element.13), channel_id=1, replica_groups=mesh['row'=32,'col'=8] {'row'}, dimensions={1}, use_global_device_ids=true | all-gather | bytes 270336 | tf_op jit(solution)/shard_map/all_gather | solution.py:75
  57.5 0.1 slice_negate_fusion.6
  57.7 37.7 %all_gather.13 = f32[3,16384]{1,0:T(4,128)S(1)} all-gather(f32[3,512]{1,0:T(4,128)} %param.12), channel_id=1, replica_groups=mesh['row'=32,'col'=8] {'row'}, dimensions={1}, use_global_device_ids=true | all-gather | bytes 202752 | tf_op jit(solution)/shard_map/all_gather | solution.py:77
  95.4 0.1 fusion.168
  95.5 40.5 %all_gather.14 = f32[3,16384]{1,0:T(4,128)S(1)} all-gather(f32[3,512]{1,0:T(4,128)} %param.13), channel_id=1, replica_groups=mesh['row'=32,'col'=8] {'row'}, dimensions={1}, use_global_device_ids=true | all-gather | bytes 202752 | tf_op jit(solution)/shard_map/all_gather | solution.py:78
  136.0 0.1 fusion.169
  136.2 0.0 copy-done
  136.2 0.1 constant_dynamic-slice_fusion
  136.3 0.0 copy-done.2
  136.3 0.0 copy-done.3
  136.3 0.0 copy-done.1
  136.4 0.1 copy.44
  136.5 0.1 copy.45
  136.6 4.4 scatter_custom_fusion
  141.1 7.1 %scatter_fusion = f32[8,8192]{0,1:T(8,128)} fusion(f32[8,8192]{0,1:T(8,128)} %scatter_custom_fusion, s32[512]{0:T(512)S(1)} %bitcast.100, f32[512,8]{1,0:T(8,128)S(1)} %copy.45), kind=kCustom, calls=%fused_computation.3 | custom fusion | flops 4096 | bytes 51200 | tf_op jit(solution)/shard_map/scatter-add | solution.py:84
  148.2 2.8 copy.46
  151.0 124.7 %all-reduce.2 = bf16[8,8192]{1,0:T(8,128)(2,1)S(1)} all-reduce(f32[8,8192]{1,0:T(8,128)S(1)} %copy.46), channel_id=1, replica_groups=mesh['row'=32,'col'=8] {'row'}, use_global_device_ids=true, to_apply=%region_3.4 | all-reduce | flops 65536 | bytes 393216 | tf_op jit(solution)/shard_map/psum | solution.py:86
  275.7 0.1 slice_negate_fusion.2
  275.7 18.1 %multiply_convert_fusion.7 = (bf16[256,2048]{1,0:T(8,128)(2,1)S(1)}, bf16[256,2048]{1,0:T(8,128)(2,1)S(1)}, bf16[256,2048]{1,0:T(8,128)(2,1)S(1)}, bf16[256,2048]{1,0:T(8,128)(2,1)S(1)}) fusion(f32[2048]{0:T(1024)S(1)} %bitcast.146, f32[2048]{0:T(1024)S(1)} %bitcast.147, f32[2048]{0:T(1024)S(1)} %bitcast.148, f32[2048]{0:T(1024)S(1)} %bitcast.136, ...), kind=kLoop, calls=%fused_computation.54 | loop fusion | flops 24117248 | bytes 4298752 | tf_op jit(solution)/shard_map/convert.14
  293.9 0.6 fusion
  294.5 18.5 %multiply_convert_fusion.1 = (bf16[256,2048]{1,0:T(8,128)(2,1)S(1)}, bf16[256,2048]{1,0:T(8,128)(2,1)S(1)}, bf16[256,2048]{1,0:T(8,128)(2,1)S(1)}, bf16[256,2048]{1,0:T(8,128)(2,1)S(1)}) fusion(f32[2048]{0:T(1024)S(1)} %bitcast.140, f32[2048]{0:T(1024)S(1)} %bitcast.141, f32[2048]{0:T(1024)S(1)} %bitcast.139, f32[2048]{0:T(1024)S(1)} %bitcast.122, ...), kind=kLoop, calls=%fused_computation.39 | loop fusion | flops 24117248 | bytes 4298752 | tf_op jit(solution)/shard_map/convert.8
  313.1 0.6 fusion.52
  313.7 18.3 %multiply_convert_fusion.3 = (bf16[256,2048]{1,0:T(8,128)(2,1)S(1)}, bf16[256,2048]{1,0:T(8,128)(2,1)S(1)}, bf16[256,2048]{1,0:T(8,128)(2,1)S(1)}, bf16[256,2048]{1,0:T(8,128)(2,1)S(1)}) fusion(f32[2048]{0:T(1024)S(1)} %bitcast.125, f32[2048]{0:T(1024)S(1)} %bitcast.126, f32[2048]{0:T(1024)S(1)} %bitcast.127, f32[2048]{0:T(1024)S(1)} %bitcast.107, ...), kind=kLoop, calls=%fused_computation.44 | loop fusion | flops 24117248 | bytes 4298752 | tf_op jit(solution)/shard_map/convert.10
  332.0 0.6 fusion.49
  332.6 18.3 %multiply_convert_fusion.5 = (bf16[256,2048]{1,0:T(8,128)(2,1)S(1)}, bf16[256,2048]{1,0:T(8,128)(2,1)S(1)}, bf16[256,2048]{1,0:T(8,128)(2,1)S(1)}, bf16[256,2048]{1,0:T(8,128)(2,1)S(1)}) fusion(f32[2048]{0:T(1024)S(1)} %bitcast.113, f32[2048]{0:T(1024)S(1)} %bitcast.114, f32[2048]{0:T(1024)S(1)} %bitcast.115, f32[2048]{0:T(1024)S(1)} %bitcast.101, ...), kind=kLoop, calls=%fused_computation.49 | loop fusion | flops 24117248 | bytes 4298752 | tf_op jit(solution)/shard_map/convert.12
  350.9 0.6 fusion.46
  351.6 0.7 fusion.43
  352.2 0.7 fusion.40
  352.9 0.7 fusion.37
  353.6 0.0 copy-start.4
  353.6 0.7 fusion.34
  354.2 0.0 copy-done.4
  354.3 0.0 all-to-all-done
  354.3 0.1 fusion.173
  354.3 17.3 %multiply_convert_fusion.17 = (bf16[128,2048]{1,0:T(8,128)(2,1)S(1)}, bf16[128,2048]{1,0:T(8,128)(2,1)S(1)}, bf16[128,2048]{1,0:T(8,128)(2,1)S(1)}, bf16[128,204...) fusion(f32[2048]{0:T(1024)S(1)} %bitcast.150, ...), kind=kLoop, calls=%fused_computation.102 | loop fusion | flops 16777216 | bytes 4294144 | tf_op jit(solution)/shard_map/convert
  371.6 0.4 fusion.55
  372.0 0.4 convolution_add_fusion.2
  372.4 0.4 convolution_add_fusion.1
  372.8 0.4 convolution_add_fusion
  373.2 26.1 %all-reduce = (f32[8,256]{1,0:T(8,128)S(1)}, f32[8,128]{1,0:T(8,128)S(1)}) all-reduce(f32[8,256]{1,0:T(8,128)S(1)} %fusion.34, f32[8,128]{1,0:T(8,128)S(1)} %convolution_add_fusion), channel_id=1, replica_groups=mesh['row'=32,'col'=8] {'col'}, use_global_device_ids=true, to_apply=%region_0.1 | all-reduce | flops 3072 | bytes 24576 | tf_op jit(solution)/shard_map/psum | solution.py:90
  399.3 0.1 constant_dynamic-slice_fusion.1
  399.4 50.1 %all_gather.15 = f32[8,4096]{1,0:T(8,128)S(1)} all-gather(f32[8,128]{1,0:T(8,128)S(1)} %maximum_multiply_fusion.1), channel_id=1, replica_groups=mesh['row'=32,'col'=8] {'row'}, dimensions={1}, use_global_device_ids=true | all-gather | bytes 135168 | tf_op jit(solution)/shard_map/all_gather | solution.py:95
  449.5 0.6 copy.47
  450.1 0.6 gather_fusion.1
  450.7 0.6 gather_fusion
  451.3 0.1 copy.48
  451.3 0.1 copy.50
  451.4 0.6 fusion.155
  (14 shorter events, 0.2 us)
Async XLA Ops:
  0.0 136.2 %copy-start = (s32[2,256]{1,0:T(2,128)S(1)}, s32[2,256]{1,0:T(2,128)}, u32[]{:S(2)}) copy-start(s32[2,256]{1,0:T(2,128)} %param.18) | copy-start | bytes 6148
  0.0 136.3 %copy-start.2 = (f32[3,256]{1,0:T(4,128)S(1)}, f32[3,256]{1,0:T(4,128)}, u32[]{:S(2)}) copy-start(f32[3,256]{1,0:T(4,128)} %param.16) | copy-start | bytes 9220
  0.0 136.3 %copy-start.3 = (f32[3,256]{1,0:T(4,128)S(1)}, f32[3,256]{1,0:T(4,128)}, u32[]{:S(2)}) copy-start(f32[3,256]{1,0:T(4,128)} %param.17) | copy-start | bytes 9220
  0.0 136.3 %copy-start.1 = (s32[2,512]{1,0:T(2,128)S(1)}, s32[2,512]{1,0:T(2,128)}, u32[]{:S(2)}) copy-start(s32[2,512]{1,0:T(2,128)} %param.14) | copy-start | bytes 12292
  1.4 352.8 %all-to-all-start = ((f32[32,3,256]{2,1,0:T(4,128)}), f32[32,3,256]{2,1,0:T(4,128)S(1)}, u32[]{:S(2)}, u32[]{:S(2)}) async-start(f32[32,3,256]{2,1,0:T(4,128)} %stack.2), calls=%async_computation | async-start | bytes 262144 | tf_op jit(solution)/shard_map/all_to_all | solution.py:15
  353.6 0.7 copy-start.4
